TPU v7x, 32 devices: a whole 2x2x4 slice. The times are simulated.
32 devices in a mesh: grp: 2 (over y), pb: 4 (over z), re: 2 (over x), ka: 2 (over core).
Axes of the slice: x: 2, y: 2, z: 4, core: 2. Of those that a mesh axis runs over, the one named last changes fastest.
Arguments:
- g_wann: bfloat16 [2, 1024, 128, 256], P(None, 'pb', ('grp', 're'), 'ka'), parts along dimension 2, may hold values from -0.0234375 to 0.0234375
- phonon_phase: bfloat16 [2, 2048, 1024], P(None, 'pb'), may hold values from -1 to 1, as said below
- electron_phase: bfloat16 [2, 8, 64], replicated, may hold values from -1 to 1, as said below
Outputs:
- coupling: float32 [16, 2, 2048, 256], P(('grp', 're'), None, 'pb', 'ka'), parts along dimension 0
There are 2 independent parts, one for each index of `grp`. A program takes and returns all parts, laid end to end along the dimension named above; an argument that names none is the same for every part. Nothing has to cross between parts.
Inputs may be any that keep to these rules, and one draw needn't show every extreme that they name: `phonon_phase`: entries 0 and 1 along the first dimension are the cosine and sine of one angle. `electron_phase`: entries 0 and 1 along the first dimension are the cosine and sine of one angle.
All inputs are finite; a program needn't handle non-finite values.
Results may differ from a plain program's by a relative error of at most 0.0029.
Values may be sent and summed in bfloat16 or wider, within the bound.
A program may use at most 64 MiB of HBM per device.

v0:
```python
import jax
import jax.numpy as jnp
from jax import lax
from jax.sharding import PartitionSpec as P


def electron_term(phase, wann_real, wann_imag):
    real_part = jnp.einsum(
        "ke,peb->kpb", phase[0], wann_real, preferred_element_type=jnp.float32
    ) - jnp.einsum("ke,peb->kpb", phase[1], wann_imag, preferred_element_type=jnp.float32)
    imag_part = jnp.einsum(
        "ke,peb->kpb", phase[0], wann_imag, preferred_element_type=jnp.float32
    ) + jnp.einsum("ke,peb->kpb", phase[1], wann_real, preferred_element_type=jnp.float32)
    return jnp.stack([real_part, imag_part])


def body(g_wann, phonon_phase, electron_phase):
    local_vectors = g_wann.shape[2]
    offset = lax.axis_index("re") * local_vectors
    own_phase = lax.dynamic_slice_in_dim(electron_phase, offset, local_vectors, 2)
    partial_value = electron_term(own_phase, g_wann[0], g_wann[1])
    summed = lax.psum_scatter(partial_value, "re", scatter_dimension=1, tiled=True)
    bloch = summed.astype(jnp.bfloat16)
    cos_table = phonon_phase[0]
    sin_table = phonon_phase[1]
    piece = lax.all_gather(bloch, "pb", axis=2, tiled=True)
    acc_real = jnp.einsum(
        "qp,kpb->kqb", cos_table, piece[0], preferred_element_type=jnp.float32
    ) - jnp.einsum("qp,kpb->kqb", sin_table, piece[1], preferred_element_type=jnp.float32)
    acc_imag = jnp.einsum(
        "qp,kpb->kqb", cos_table, piece[1], preferred_element_type=jnp.float32
    ) + jnp.einsum("qp,kpb->kqb", sin_table, piece[0], preferred_element_type=jnp.float32)
    acc_real, acc_imag = (acc_real, acc_imag)
    return jnp.stack([acc_real, acc_imag], axis=1)


def solution(mesh):
    placed = (P(None, "pb", ("grp", "re"), "ka"), P(None, "pb", None), P())
    return jax.shard_map(
        body,
        mesh=mesh,
        in_specs=placed,
        out_specs=P(("grp", "re"), None, "pb", "ka"),
        check_vma=False,
    )
```

profile of v0, /device:TPU:0, one launch (start us, length us, event | category | flops | bytes accessed | tf_op | source)
XLA Modules:
  0.0 110.9 jit_solution(2155230755220057174)
XLA Ops:
  6.5 0.0 copy-start
  6.5 0.0 reduce-scatter.2.cloned.1.call-start
  6.5 0.7 copy-done
  7.2 0.0 copy-start.1
  7.2 2.2 %fusion = f32[8,256,128]{2,0,1:T(8,128)S(1)} fusion(bf16[2,256,32,128]{3,2,1,0:T(8,128)(2,1)} %param.3, bf16[2,8,64]{2,1,0:T(8,128)(2,1)S(1)} %copy-done, s32[]{:T(128)S(6)} %select_n.3), kind=kOutput, calls=%fused_computation.2 | convolution fusion | flops 16777216 | bytes 3147780 | tf_op jit(solution)/shard_map/ke,peb->kpb/dot_general | solution.py:11
  9.4 2.0 %fusion.2 = f32[8,256,128]{2,0,1:T(8,128)S(1)} fusion(bf16[2,256,32,128]{3,2,1,0:T(8,128)(2,1)} %param.3, bf16[2,8,64]{2,1,0:T(8,128)(2,1)S(1)} %copy-done, s32[]{:T(128)S(6)} %add.18, s32[]{:T(128)S(6)} %select_n.3), kind=kOutput, calls=%fused_computation.4 | convolution fusion | flops 16777216 | bytes 3147784 | tf_op jit(solution)/shard_map/ke,peb->kpb/dot_general | solution.py:10
  11.5 0.0 copy-done.1
  11.5 0.5 fusion.21
  11.9 0.5 fusion.15
  12.4 0.1 pad_maximum_fusion
  12.5 1.7 %copy.9 = f32[2,8,256,128]{3,2,0,1:T(8,128)} copy(f32[2,8,256,128]{3,1,2,0:T(8,128)S(1)} %pad_maximum_fusion) | data formatting | bytes 4194304 | tf_op jit(solution)/shard_map/stack | solution.py:14
  14.2 0.0 copy-start.2
  14.2 0.0 reduce-scatter.2.cloned.1.call-update
  14.3 0.0 all-gather.2.cloned.1.call-start
  14.3 34.7 %reduce-scatter.2.cloned.1.call-done = f32[2,4,256,128]{3,2,0,1:T(8,128)} async-done(((f32[2,8,256,128]{3,2,0,1:T(8,128)}), f32[2,4,256,128]{3,2,0,1:T(8,128)}) %reduce-scatter.2.cloned.1.call-update) | async-done | bytes 1048592 | tf_op jit(solution)/shard_map/reduce_scatter | solution.py:22
  49.0 2.2 %copy.10 = bf16[2,4,256,128]{2,3,1,0:T(8,128)(2,1)} copy(f32[2,4,256,128]{3,2,0,1:T(8,128)} %reduce-scatter.2.cloned.1.call-done) | data formatting | bytes 1572864 | tf_op jit(solution)/shard_map/reduce_scatter | solution.py:22
  51.3 0.0 all-gather.2.cloned.1.call-update
  51.3 46.4 %all-gather.2.cloned.1.call-done = bf16[2,4,1024,128]{2,3,1,0:T(8,128)(2,1)} async-done(((bf16[2,4,256,128]{2,3,1,0:T(8,128)(2,1)}), bf16[2,4,1024,128]{2,3,1,0:T(8,128)(2,1)}) %all-gather.2.cloned.1.call-update) | async-done | bytes 2097168 | tf_op jit(solution)/shard_map/all_gather | solution.py:26
  97.7 0.0 copy-done.2
  97.7 0.0 copy-start.3
  97.7 2.1 %fusion.28 = f32[4,128,512]{2,1,0:T(8,128)S(1)} fusion(bf16[2,4,1024,128]{2,3,1,0:T(8,128)(2,1)} %all-gather.2.cloned.1.call-done, bf16[2,512,1024]{2,1,0:T(8,128)(2,1)S(1)} %copy-done.2), kind=kOutput, calls=%fused_computation.26 | convolution fusion | flops 536870912 | bytes 3145728 | tf_op jit(solution)/shard_map/qp,kpb->kqb/dot_general | solution.py:30
  99.8 0.0 copy-done.3
  99.8 0.7 fusion.30
  100.6 0.7 fusion.24
  101.3 0.7 fusion.25
  102.1 0.2 pad_maximum_fusion.1
  102.3 1.8 %copy.11 = f32[4,2,512,128]{3,2,1,0:T(8,128)} copy(f32[4,2,512,128]{2,3,0,1:T(8,128)S(1)} %pad_maximum_fusion.1) | data formatting | bytes 4194304 | tf_op jit(solution)/shard_map/stack | solution.py:34
Async XLA Ops:
  6.5 0.7 copy-start
  6.5 42.5 %reduce-scatter.2.cloned.1.call-start = ((), (), s32[]{:S(2)}) async-start(), calls=%async_computation.1 | async-start | bytes 3145728 | tf_op jit(solution)/shard_map/reduce_scatter | solution.py:22
  7.2 4.2 %copy-start.1 = (bf16[2,256,32,128]{3,2,1,0:T(8,128)(2,1)S(1)}, bf16[2,256,32,128]{3,2,1,0:T(8,128)(2,1)}, u32[]{:S(2)}) copy-start(bf16[2,256,32,128]{3,2,1,0:T(8,128)(2,1)} %param.3) | copy-start | bytes 12582916
  14.2 83.5 %copy-start.2 = (bf16[2,512,1024]{2,1,0:T(8,128)(2,1)S(1)}, bf16[2,512,1024]{2,1,0:T(8,128)(2,1)}, u32[]{:S(2)}) copy-start(bf16[2,512,1024]{2,1,0:T(8,128)(2,1)} %param.4) | copy-start | bytes 6291460
  14.3 83.4 %all-gather.2.cloned.1.call-start = ((), (), s32[]{:S(2)}) async-start(), calls=%async_computation.2 | async-start | bytes 2621440 | tf_op jit(solution)/shard_map/all_gather | solution.py:26
  97.7 2.1 %copy-start.3 = (bf16[2,4,1024,128]{2,3,1,0:T(8,128)(2,1)S(1)}, bf16[2,4,1024,128]{2,3,1,0:T(8,128)(2,1)}, u32[]{:S(2)}) copy-start(bf16[2,4,1024,128]{2,3,1,0:T(8,128)(2,1)} %all-gather.2.cloned.1.call-done) | copy-start | bytes 6291460
Sparse Core Ops, SparseCore 0:
  14.4 34.6 reduce-scatter.1
  51.4 46.2 all-gather.1
where the time goes:
time: 111 us
  waiting for transfers between devices  81.2 us (73%)
  between operations  13.5 us (12%)
  matrix products  9.5 us (9%)
  local copies, waits for them, and re-layouts  6.43 us (6%)
    all_gather x1, waiting for transfers between devices, body(): piece = lax.all_gather(bloch, 'pb', axis=2, tiled=True)  46.4 us
    reduce_scatter x1, waiting for transfers between devices, body(): lax.psum_scatter(partial_value, 're', scatter_dimension=1, tiled=True)  34.7 us
    reduce_scatter x1, local copies, waits for them, and re-layouts, body(): lax.psum_scatter(partial_value, 're', scatter_dimension=1, tiled=True)  2.22 us
  transfers between devices with their start and end apart: 2, of which 2 were waited for; matrix products, arithmetic and copies ran while one was open for 0% of the time, Pallas kernels for 0%

commit v1 on v0

--- a/solution.py
+++ b/solution.py
@@ -2,6 +2,18 @@
 import jax.numpy as jnp
 from jax import lax
 from jax.sharding import PartitionSpec as P
+
+
+def gather_by_bits(x, axis, dim):
+    ways, here = (lax.axis_size(axis), lax.axis_index(axis))
+    grown, reach = (x, 1)
+    while reach < ways:
+        theirs = lax.ppermute(grown, axis, [(d, d ^ reach) for d in range(ways)])
+        mine_first = jnp.concatenate([grown, theirs], axis=dim)
+        theirs_first = jnp.concatenate([theirs, grown], axis=dim)
+        grown = jnp.where(here & reach == 0, mine_first, theirs_first)
+        reach = 2 * reach
+    return grown
 
 
 def electron_term(phase, wann_real, wann_imag):
@@ -23,7 +35,7 @@
     bloch = summed.astype(jnp.bfloat16)
     cos_table = phonon_phase[0]
     sin_table = phonon_phase[1]
-    piece = lax.all_gather(bloch, "pb", axis=2, tiled=True)
+    piece = gather_by_bits(bloch, "pb", 2)
     acc_real = jnp.einsum(
         "qp,kpb->kqb", cos_table, piece[0], preferred_element_type=jnp.float32
     ) - jnp.einsum("qp,kpb->kqb", sin_table, piece[1], preferred_element_type=jnp.float32)

time: 111 us -> 124 us (1.12)
  waiting for transfers between devices: 81.2 us -> 91.7 us
  starting transfers between devices: 0.04 us -> 4.01 us
  matrix products: 9.5 us -> 8.11 us
    ppermute x0 -> x2, waiting for transfers between devices: none -> 56.9 us  [gather_by_bits(): theirs = lax.ppermute(grown, axis, [(d, d ^ reach) for d in range(ways)])]
    all_gather x1 -> x0, waiting for transfers between devices: 46.4 us -> none  [body(): piece = lax.all_gather(bloch, 'pb', axis=2, tiled=True)]
    ppermute x0 -> x2, starting transfers between devices: none -> 4.01 us  [gather_by_bits(): theirs = lax.ppermute(grown, axis, [(d, d ^ reach) for d in range(ways)])]
    dot_general x1, matrix products: 2.12 us -> 0.74 us  [body(): jnp.einsum('qp,kpb->kqb', cos_table, piece[1], preferred_element_type=jnp...]
  transfers between devices with their start and end apart: 2 -> 3, of which waited for: 2 -> 3; matrix products, arithmetic and copies ran while one was open for 0% -> 0% of each run, Pallas kernels for 0% -> 0%
where the time goes in v1:
time: 124 us
  waiting for transfers between devices  91.7 us (74%)
  between operations  13.5 us (11%)
  matrix products  8.11 us (7%)
  local copies, waits for them, and re-layouts  5.63 us (5%)
  starting transfers between devices  4.01 us (3%)
  other arithmetic  1.24 us (1%)
    ppermute x2, waiting for transfers between devices, gather_by_bits(): theirs = lax.ppermute(grown, axis, [(d, d ^ reach) for d in range(ways)])  56.9 us
    reduce_scatter x1, waiting for transfers between devices, body(): lax.psum_scatter(partial_value, 're', scatter_dimension=1, tiled=True)  34.8 us
    ppermute x2, starting transfers between devices, gather_by_bits(): theirs = lax.ppermute(grown, axis, [(d, d ^ reach) for d in range(ways)])  4.01 us
  transfers between devices with their start and end apart: 3, of which 3 were waited for; matrix products, arithmetic and copies ran while one was open for 0% of the time, Pallas kernels for 0%

profile of v1, /device:TPU:0, one launch (start us, length us, event | category | flops | bytes accessed | tf_op | source)
XLA Modules:
  0.0 124.1 jit_solution(8773569732101580187)
XLA Ops:
  6.5 0.0 copy-start
  6.5 0.0 reduce-scatter.2.cloned.1.call-start
  6.5 0.7 copy-done
  7.2 0.0 copy-start.1
  7.2 2.2 %fusion = f32[8,256,128]{2,0,1:T(8,128)S(1)} fusion(bf16[2,256,32,128]{3,2,1,0:T(8,128)(2,1)} %param.3, bf16[2,8,64]{2,1,0:T(8,128)(2,1)S(1)} %copy-done, s32[]{:T(128)S(6)} %select_n.21), kind=kOutput, calls=%fused_computation.3 | convolution fusion | flops 16777216 | bytes 3147780 | tf_op jit(solution)/shard_map/ke,peb->kpb/dot_general | solution.py:23
  9.4 2.0 %fusion.2 = f32[8,256,128]{2,0,1:T(8,128)S(1)} fusion(bf16[2,256,32,128]{3,2,1,0:T(8,128)(2,1)} %param.3, bf16[2,8,64]{2,1,0:T(8,128)(2,1)S(1)} %copy-done, s32[]{:T(128)S(6)} %add.18, s32[]{:T(128)S(6)} %select_n.21), kind=kOutput, calls=%fused_computation.5 | convolution fusion | flops 16777216 | bytes 3147784 | tf_op jit(solution)/shard_map/ke,peb->kpb/dot_general | solution.py:22
  11.5 0.0 copy-done.1
  11.5 0.5 fusion.15
  11.9 0.5 fusion.21
  12.4 0.1 pad_maximum_fusion
  12.5 1.7 %copy.9 = f32[2,8,256,128]{3,2,0,1:T(8,128)} copy(f32[2,8,256,128]{3,1,2,0:T(8,128)S(1)} %pad_maximum_fusion) | data formatting | bytes 4194304 | tf_op jit(solution)/shard_map/stack | solution.py:26
  14.2 0.0 reduce-scatter.2.cloned.1.call-update
  14.3 34.8 %reduce-scatter.2.cloned.1.call-done = f32[2,4,256,128]{3,2,0,1:T(8,128)} async-done(((f32[2,8,256,128]{3,2,0,1:T(8,128)}), f32[2,4,256,128]{3,2,0,1:T(8,128)}) %reduce-scatter.2.cloned.1.call-update) | async-done | bytes 1048592 | tf_op jit(solution)/shard_map/reduce_scatter | solution.py:34
  49.0 1.4 %copy.10 = bf16[2,4,256,128]{2,3,1,0:T(8,128)(2,1)S(1)} copy(f32[2,4,256,128]{3,2,0,1:T(8,128)} %reduce-scatter.2.cloned.1.call-done) | data formatting | bytes 1572864 | tf_op jit(solution)/shard_map/reduce_scatter | solution.py:34
  50.5 1.5 %collective-permute-start = (bf16[2,4,256,128]{2,3,1,0:T(8,128)(2,1)S(1)}, bf16[2,4,256,128]{2,3,1,0:T(8,128)(2,1)S(1)}, u32[]{:S(2)}, u32[]{:S(2)}) collective-permute-start(bf16[2,4,256,128]{2,3,1,0:T(8,128)(2,1)S(1)} %copy.10), channel_id=1, source_target_pairs={{0,4},{4,0},{8,12},{12,8},{1,5},{5,1},{9,13},{13,9},{2,6},{6,2},{1... | collective-permute-start | bytes 1572872 | tf_op jit(solution)/shard_map/ppermute | solution.py:11
  52.0 12.0 %collective-permute-done = bf16[2,4,256,128]{2,3,1,0:T(8,128)(2,1)S(1)} collective-permute-done((bf16[2,4,256,128]{2,3,1,0:T(8,128)(2,1)S(1)}, bf16[2,4,256,128]{2,3,1,0:T(8,128)(2,1)S(1)}, u32[]{:S(2)}, u32[]{:S(2)}) %collective-permute-start) | collective-permute-done | bytes 524320 | tf_op jit(solution)/shard_map/ppermute | solution.py:11
  64.0 0.3 maximum_select_fusion.1
  64.3 2.5 %collective-permute-start.1 = (bf16[2,4,512,128]{2,3,1,0:T(8,128)(2,1)S(1)}, bf16[2,4,512,128]{2,3,1,0:T(8,128)(2,1)S(1)}, u32[]{:S(2)}, u32[]{:S(2)}) collective-permute-start(bf16[2,4,512,128]{2,3,1,0:T(8,128)(2,1)S(1)} %maximum_select_fusion.1), channel_id=1, source_target_pairs={{0,8},{4,12},{8,0},{12,4},{1,9},{5,13},{9,1},{13,5},{2,10},{6,14},... | collective-permute-start | bytes 3145736 | tf_op jit(solution)/shard_map/ppermute | solution.py:11
  66.8 0.0 copy-start.2
  66.8 44.9 %collective-permute-done.1 = bf16[2,4,512,128]{2,3,1,0:T(8,128)(2,1)S(1)} collective-permute-done((bf16[2,4,512,128]{2,3,1,0:T(8,128)(2,1)S(1)}, bf16[2,4,512,128]{2,3,1,0:T(8,128)(2,1)S(1)}, u32[]{:S(2)}, u32[]{:S(2)}) %collective-permute-start.1) | collective-permute-done | bytes 1048608 | tf_op jit(solution)/shard_map/ppermute | solution.py:11
  111.6 0.7 maximum_select_fusion
  112.3 0.0 copy-done.2
  112.3 0.7 fusion.28
  113.1 0.7 fusion.26
  113.8 0.7 fusion.25
  114.6 0.7 fusion.24
  115.3 0.2 pad_maximum_fusion.1
  115.5 1.8 %copy.11 = f32[4,2,512,128]{3,2,1,0:T(8,128)} copy(f32[4,2,512,128]{2,3,0,1:T(8,128)S(1)} %pad_maximum_fusion.1) | data formatting | bytes 4194304 | tf_op jit(solution)/shard_map/stack | solution.py:46
Async XLA Ops:
  6.5 0.7 copy-start
  6.5 42.5 %reduce-scatter.2.cloned.1.call-start = ((), (), s32[]{:S(2)}) async-start(), calls=%async_computation.1 | async-start | bytes 3145728 | tf_op jit(solution)/shard_map/reduce_scatter | solution.py:34
  7.2 4.2 %copy-start.1 = (bf16[2,256,32,128]{3,2,1,0:T(8,128)(2,1)S(1)}, bf16[2,256,32,128]{3,2,1,0:T(8,128)(2,1)}, u32[]{:S(2)}) copy-start(bf16[2,256,32,128]{3,2,1,0:T(8,128)(2,1)} %param.3) | copy-start | bytes 12582916
  50.5 13.6 %collective-permute-start = (bf16[2,4,256,128]{2,3,1,0:T(8,128)(2,1)S(1)}, bf16[2,4,256,128]{2,3,1,0:T(8,128)(2,1)S(1)}, u32[]{:S(2)}, u32[]{:S(2)}) collective-permute-start(bf16[2,4,256,128]{2,3,1,0:T(8,128)(2,1)S(1)} %copy.10), channel_id=1, source_target_pairs={{0,4},{4,0},{8,12},{12,8},{1,5},{5,1},{9,13},{13,9},{2,6},{6,2},{1... | collective-permute-start | bytes 1572872 | tf_op jit(solution)/shard_map/ppermute | solution.py:11
  64.3 47.3 %collective-permute-start.1 = (bf16[2,4,512,128]{2,3,1,0:T(8,128)(2,1)S(1)}, bf16[2,4,512,128]{2,3,1,0:T(8,128)(2,1)S(1)}, u32[]{:S(2)}, u32[]{:S(2)}) collective-permute-start(bf16[2,4,512,128]{2,3,1,0:T(8,128)(2,1)S(1)} %maximum_select_fusion.1), channel_id=1, source_target_pairs={{0,8},{4,12},{8,0},{12,4},{1,9},{5,13},{9,1},{13,5},{2,10},{6,14},... | collective-permute-start | bytes 3145736 | tf_op jit(solution)/shard_map/ppermute | solution.py:11
  66.8 45.5 %copy-start.2 = (bf16[2,512,1024]{2,1,0:T(8,128)(2,1)S(1)}, bf16[2,512,1024]{2,1,0:T(8,128)(2,1)}, u32[]{:S(2)}) copy-start(bf16[2,512,1024]{2,1,0:T(8,128)(2,1)} %param.4) | copy-start | bytes 6291460
Sparse Core Ops, SparseCore 0:
  14.4 34.6 reduce-scatter.1
